TPU v7x, 32 devices: a whole 2x2x4 slice. The times are simulated.
32 devices in a mesh: ctx: 16 (over z, y, x), fsdp: 2 (over core).
Axes of the slice: x: 2, y: 2, z: 4, core: 2. Of those that a mesh axis runs over, the one named last changes fastest.
Arguments:
- block_input: bfloat16 [4, 1024, 1024], P('fsdp', 'ctx'), may hold values from -6 to 6
- cotangent: bfloat16 [4, 1024, 1024], P('fsdp', 'ctx'), may hold values from -6 to 6
- block_table: int32 [16, 2], replicated, may hold values from 0 to 31, as said below
- segments: int32 [4, 1024], P('fsdp'), may hold values from 0 to 2, as said below
- gain_one: bfloat16 [1024], P('fsdp'), may hold values from 0.25 to 1.75
- shift_one: bfloat16 [1024], P('fsdp'), may hold values from -3 to 3
- w_mix: bfloat16 [1024, 3072], P('fsdp'), may hold values from -0.1875 to 0.1875
- bias_query: bfloat16 [1024], P('fsdp'), may hold values from -3 to 3
- bias_value: bfloat16 [1024], P('fsdp'), may hold values from -3 to 3
- w_merge: bfloat16 [1024, 1024], P('fsdp'), may hold values from -0.375 to 0.375
- bias_merge: bfloat16 [1024], P('fsdp'), may hold values from -3 to 3
- gain_two: bfloat16 [1024], P('fsdp'), may hold values from 0.25 to 1.75
- shift_two: bfloat16 [1024], P('fsdp'), may hold values from -3 to 3
- w_expand: bfloat16 [1024, 4096], P('fsdp'), may hold values from -0.1875 to 0.1875
- bias_expand: bfloat16 [4096], P('fsdp'), may hold values from -3 to 3
- w_reduce: bfloat16 [4096, 1024], P('fsdp'), may hold values from -0.09375 to 0.09375
- bias_reduce: bfloat16 [1024], P('fsdp'), may hold values from -3 to 3
Outputs:
- block_output: bfloat16 [4, 1024, 1024], P('fsdp', 'ctx')
- grad_input: float32 [4, 1024, 1024], P('fsdp', 'ctx')
- grad_gain_one: float32 [1024], P(('ctx', 'fsdp'))
- grad_shift_one: float32 [1024], P(('ctx', 'fsdp'))
- grad_w_mix: float32 [1024, 3072], P(('ctx', 'fsdp'))
- grad_bias_query: float32 [1024], P(('ctx', 'fsdp'))
- grad_bias_value: float32 [1024], P(('ctx', 'fsdp'))
- grad_w_merge: float32 [1024, 1024], P(('ctx', 'fsdp'))
- grad_bias_merge: float32 [1024], P(('ctx', 'fsdp'))
- grad_gain_two: float32 [1024], P(('ctx', 'fsdp'))
- grad_shift_two: float32 [1024], P(('ctx', 'fsdp'))
- grad_w_expand: float32 [1024, 4096], P(('ctx', 'fsdp'))
- grad_bias_expand: float32 [4096], P(('ctx', 'fsdp'))
- grad_w_reduce: float32 [4096, 1024], P(('ctx', 'fsdp'))
- grad_bias_reduce: float32 [1024], P(('ctx', 'fsdp'))
Inputs may be any that keep to these rules, and one draw needn't show every extreme that they name: `block_table`: row c lists the two blocks of 32 positions that the slots of index c of ctx hold, in slot order: a block b below 16, then its mirror 2 * 16 - 1 - b; every block appears once. `segments`: document ids by slot. Taken in order of position (slot s holds position block_table[s // 64, (s // 32) % 2] * 32 + s % 32), the ids of a sequence never fall, and each of its 3 documents holds at least one position.
All inputs are finite; a program needn't handle non-finite values.
Results may differ from a plain program's by a relative error of at most 0.02.
Values may be sent and summed in bfloat16 or wider, within the bound.
A program may use at most 320 MiB of HBM per device.

v0:
```python
import math
import jax
import jax.numpy as jnp
from jax import lax
from jax.sharding import PartitionSpec as P

HEADS = 16
EPSILON = 1e-05
CUBIC = 0.044715
ROOT = math.sqrt(2.0 / math.pi)


def gelu_value(pre):
    inner = ROOT * (pre + CUBIC * pre * pre * pre)
    return 0.5 * pre * (1.0 + jnp.tanh(inner))


def gelu_slope(pre):
    inner = ROOT * (pre + CUBIC * pre * pre * pre)
    tangent = jnp.tanh(inner)
    return 0.5 * (1.0 + tangent) + 0.5 * pre * (1.0 - tangent * tangent) * ROOT * (
        1.0 + 3.0 * CUBIC * pre * pre
    )


def norm_forward(rows, gain, shift):
    center = rows - jnp.mean(rows, axis=-1, keepdims=True)
    inverse = lax.rsqrt(jnp.mean(center * center, axis=-1, keepdims=True) + EPSILON)
    normed = center * inverse
    return (
        normed,
        inverse,
        (normed * gain.astype(jnp.float32) + shift.astype(jnp.float32)).astype(jnp.bfloat16),
    )


def norm_backward(grad, normed, inverse, gain):
    scaled = grad * gain.astype(jnp.float32)
    return inverse * (
        scaled
        - jnp.mean(scaled, axis=-1, keepdims=True)
        - normed * jnp.mean(scaled * normed, axis=-1, keepdims=True)
    )


def slot_positions(block_table, block):
    blocks = block_table.reshape(-1)
    return (blocks[:, None] * block + jnp.arange(block, dtype=jnp.int32)[None, :]).reshape(-1)


def body(
    block_input,
    cotangent,
    block_table,
    segments,
    gain_one,
    shift_one,
    w_mix,
    bias_query,
    bias_value,
    w_merge,
    bias_merge,
    gain_two,
    shift_two,
    w_expand,
    bias_expand,
    w_reduce,
    bias_reduce,
):
    groups, width, model = block_input.shape
    length = segments.shape[1]
    heads = HEADS
    head = model // heads
    half_heads = heads // 2
    scale = 1.0 / math.sqrt(head)
    (
        gain_one,
        shift_one,
        w_mix,
        bias_query,
        bias_value,
        w_merge,
        bias_merge,
        gain_two,
        shift_two,
        w_expand,
        bias_expand,
        w_reduce,
        bias_reduce,
    ) = (
        lax.all_gather(gain_one, "fsdp", axis=0, tiled=True),
        lax.all_gather(shift_one, "fsdp", axis=0, tiled=True),
        lax.all_gather(w_mix, "fsdp", axis=0, tiled=True),
        lax.all_gather(bias_query, "fsdp", axis=0, tiled=True),
        lax.all_gather(bias_value, "fsdp", axis=0, tiled=True),
        lax.all_gather(w_merge, "fsdp", axis=0, tiled=True),
        lax.all_gather(bias_merge, "fsdp", axis=0, tiled=True),
        lax.all_gather(gain_two, "fsdp", axis=0, tiled=True),
        lax.all_gather(shift_two, "fsdp", axis=0, tiled=True),
        lax.all_gather(w_expand, "fsdp", axis=0, tiled=True),
        lax.all_gather(bias_expand, "fsdp", axis=0, tiled=True),
        lax.all_gather(w_reduce, "fsdp", axis=0, tiled=True),
        lax.all_gather(bias_reduce, "fsdp", axis=0, tiled=True),
    )
    key_position = slot_positions(block_table, width // 2)
    first_slot = lax.axis_index("ctx") * width
    query_position = lax.dynamic_slice_in_dim(key_position, first_slot, width)
    query_segment = lax.dynamic_slice_in_dim(segments, first_slot, width, axis=1)
    visible = jnp.logical_and(
        key_position[None, None, :] <= query_position[None, :, None],
        segments[:, None, :] == query_segment[:, :, None],
    )
    tokens = block_input.reshape(groups * width, model).astype(jnp.float32)
    normed_one, inverse_one, first_in = norm_forward(tokens, gain_one, shift_one)
    offsets = jnp.concatenate([bias_query, jnp.zeros_like(bias_query), bias_value]).astype(
        jnp.float32
    )
    mixed = (jnp.dot(first_in, w_mix, preferred_element_type=jnp.float32) + offsets).astype(
        jnp.bfloat16
    )
    queries = mixed[:, :model].reshape(groups, width, heads, head)
    local_pairs = mixed[:, model:].reshape(groups, width, 2 * model)
    pairs = lax.all_gather(local_pairs, "ctx", axis=1, tiled=True)
    keys = pairs[:, :, :model].reshape(groups, length, heads, head)
    values = pairs[:, :, model:].reshape(groups, length, heads, head)
    context_parts, log_parts = ([], [])
    for half in range(2):
        first = half * half_heads
        part_scores = (
            jnp.einsum(
                "gshd,gthd->ghst",
                queries[:, :, first : first + half_heads],
                keys[:, :, first : first + half_heads],
                preferred_element_type=jnp.float32,
            )
            * scale
        )
        expo = jnp.where(visible[:, None], jnp.exp(part_scores), 0.0)
        total = jnp.sum(expo, axis=-1)
        summed = jnp.einsum(
            "ghst,gthd->gshd",
            expo.astype(jnp.bfloat16),
            values[:, :, first : first + half_heads],
            preferred_element_type=jnp.float32,
        )
        context_parts.append(summed / jnp.swapaxes(total, 1, 2)[..., None])
        log_parts.append(jnp.log(total))
    context = jnp.concatenate(context_parts, axis=2).astype(jnp.bfloat16)
    log_total = jnp.concatenate(log_parts, axis=1)
    context_rows = context.reshape(groups * width, model)
    resid = (
        tokens
        + jnp.dot(context_rows, w_merge, preferred_element_type=jnp.float32)
        + bias_merge.astype(jnp.float32)
    )
    normed_two, inverse_two, second_in = norm_forward(resid, gain_two, shift_two)
    pre = jnp.dot(second_in, w_expand, preferred_element_type=jnp.float32) + bias_expand.astype(
        jnp.float32
    )
    act = gelu_value(pre).astype(jnp.bfloat16)
    block_output = (
        resid
        + jnp.dot(act, w_reduce, preferred_element_type=jnp.float32)
        + bias_reduce.astype(jnp.float32)
    ).astype(jnp.bfloat16)
    upstream = cotangent.reshape(groups * width, model)
    incoming = upstream.astype(jnp.float32)
    grad_reduce = jnp.einsum("ti,tj->ij", act, upstream, preferred_element_type=jnp.float32)
    grad_pre = jnp.einsum(
        "tj,ij->ti", upstream, w_reduce, preferred_element_type=jnp.float32
    ) * gelu_slope(pre)
    pre_rounded = grad_pre.astype(jnp.bfloat16)
    grad_expand = jnp.einsum(
        "ti,tj->ij", second_in, pre_rounded, preferred_element_type=jnp.float32
    )
    grad_second = jnp.einsum("tj,ij->ti", pre_rounded, w_expand, preferred_element_type=jnp.float32)
    grad_resid = incoming + norm_backward(grad_second, normed_two, inverse_two, gain_two)
    feed = (
        lax.psum_scatter(
            jnp.sum(grad_second * normed_two, axis=0),
            ("ctx", "fsdp"),
            scatter_dimension=0,
            tiled=True,
        ),
        lax.psum_scatter(
            jnp.sum(grad_second, axis=0), ("ctx", "fsdp"), scatter_dimension=0, tiled=True
        ),
        lax.psum_scatter(grad_expand, ("ctx", "fsdp"), scatter_dimension=0, tiled=True),
        lax.psum_scatter(
            jnp.sum(grad_pre, axis=0), ("ctx", "fsdp"), scatter_dimension=0, tiled=True
        ),
        lax.psum_scatter(grad_reduce, ("ctx", "fsdp"), scatter_dimension=0, tiled=True),
        lax.psum_scatter(
            jnp.sum(incoming, axis=0), ("ctx", "fsdp"), scatter_dimension=0, tiled=True
        ),
    )
    resid_rounded = grad_resid.astype(jnp.bfloat16)
    grad_merge = jnp.einsum(
        "ti,tj->ij", context_rows, resid_rounded, preferred_element_type=jnp.float32
    )
    grad_context = jnp.einsum(
        "tj,ij->ti", resid_rounded, w_merge, preferred_element_type=jnp.float32
    ).astype(jnp.bfloat16)
    delta = jnp.sum(
        (grad_context.astype(jnp.float32) * context_rows.astype(jnp.float32)).reshape(
            groups, width, heads, head
        ),
        axis=-1,
    )
    delta = jnp.swapaxes(delta, 1, 2)
    grad_heads = grad_context.reshape(groups, width, heads, head)
    query_parts, key_parts, value_parts = ([], [], [])
    for half in range(2):
        first = half * half_heads
        query_part = queries[:, :, first : first + half_heads]
        key_part = keys[:, :, first : first + half_heads]
        value_part = values[:, :, first : first + half_heads]
        grad_part = grad_heads[:, :, first : first + half_heads]
        part_scores = (
            jnp.einsum("gshd,gthd->ghst", query_part, key_part, preferred_element_type=jnp.float32)
            * scale
        )
        prob = jnp.where(
            visible[:, None],
            jnp.exp(part_scores - log_total[:, first : first + half_heads, :, None]),
            0.0,
        )
        dprob = jnp.einsum(
            "gshd,gthd->ghst", grad_part, value_part, preferred_element_type=jnp.float32
        )
        grad_score = prob * (dprob - delta[:, first : first + half_heads, :, None])
        score_rounded = grad_score.astype(jnp.bfloat16)
        query_parts.append(
            jnp.einsum(
                "ghst,gthd->gshd", score_rounded, key_part, preferred_element_type=jnp.float32
            )
            * scale
        )
        key_term = (
            jnp.einsum(
                "ghst,gshd->gthd", score_rounded, query_part, preferred_element_type=jnp.float32
            )
            * scale
        )
        value_term = jnp.einsum(
            "ghst,gshd->gthd",
            prob.astype(jnp.bfloat16),
            grad_part,
            preferred_element_type=jnp.float32,
        )
        key_sum, value_sum = (
            lax.psum_scatter(
                key_term.reshape(groups, length, half_heads * head),
                "ctx",
                scatter_dimension=1,
                tiled=True,
            ),
            lax.psum_scatter(
                value_term.reshape(groups, length, half_heads * head),
                "ctx",
                scatter_dimension=1,
                tiled=True,
            ),
        )
        key_parts.append(key_sum)
        value_parts.append(value_sum)
    grad_query = jnp.concatenate(query_parts, axis=2)
    grad_key = jnp.concatenate(key_parts, axis=2)
    grad_value = jnp.concatenate(value_parts, axis=2)
    query_rows_grad = grad_query.reshape(groups * width, model)
    key_rows_grad = grad_key.reshape(groups * width, model)
    value_rows_grad = grad_value.reshape(groups * width, model)
    grad_mixed = jnp.concatenate([query_rows_grad, key_rows_grad, value_rows_grad], axis=1).astype(
        jnp.bfloat16
    )
    grad_mix = jnp.einsum("ti,tj->ij", first_in, grad_mixed, preferred_element_type=jnp.float32)
    grad_first = jnp.einsum("tj,ij->ti", grad_mixed, w_mix, preferred_element_type=jnp.float32)
    grad_tokens = grad_resid + norm_backward(grad_first, normed_one, inverse_one, gain_one)
    front = (
        lax.psum_scatter(
            jnp.sum(grad_first * normed_one, axis=0),
            ("ctx", "fsdp"),
            scatter_dimension=0,
            tiled=True,
        ),
        lax.psum_scatter(
            jnp.sum(grad_first, axis=0), ("ctx", "fsdp"), scatter_dimension=0, tiled=True
        ),
        lax.psum_scatter(grad_mix, ("ctx", "fsdp"), scatter_dimension=0, tiled=True),
        lax.psum_scatter(
            jnp.sum(query_rows_grad, axis=0), ("ctx", "fsdp"), scatter_dimension=0, tiled=True
        ),
        lax.psum_scatter(
            jnp.sum(value_rows_grad, axis=0), ("ctx", "fsdp"), scatter_dimension=0, tiled=True
        ),
        lax.psum_scatter(grad_merge, ("ctx", "fsdp"), scatter_dimension=0, tiled=True),
        lax.psum_scatter(
            jnp.sum(grad_resid, axis=0), ("ctx", "fsdp"), scatter_dimension=0, tiled=True
        ),
    )
    return (
        block_output.reshape(groups, width, model),
        grad_tokens.reshape(groups, width, model),
        front[0],
        front[1],
        front[2],
        front[3],
        front[4],
        front[5],
        front[6],
        feed[0],
        feed[1],
        feed[2],
        feed[3],
        feed[4],
        feed[5],
    )


def solution(mesh):
    in_specs = (
        P("fsdp", "ctx", None),
        P("fsdp", "ctx", None),
        P(),
        P("fsdp", None),
        P("fsdp"),
        P("fsdp"),
        P("fsdp", None),
        P("fsdp"),
        P("fsdp"),
        P("fsdp", None),
        P("fsdp"),
        P("fsdp"),
        P("fsdp"),
        P("fsdp", None),
        P("fsdp"),
        P("fsdp", None),
        P("fsdp"),
    )
    out_specs = (
        P("fsdp", "ctx", None),
        P("fsdp", "ctx", None),
        P(("ctx", "fsdp")),
        P(("ctx", "fsdp")),
        P(("ctx", "fsdp"), None),
        P(("ctx", "fsdp")),
        P(("ctx", "fsdp")),
        P(("ctx", "fsdp"), None),
        P(("ctx", "fsdp")),
        P(("ctx", "fsdp")),
        P(("ctx", "fsdp")),
        P(("ctx", "fsdp"), None),
        P(("ctx", "fsdp")),
        P(("ctx", "fsdp"), None),
        P(("ctx", "fsdp")),
    )
    return jax.shard_map(body, mesh=mesh, in_specs=in_specs, out_specs=out_specs, check_vma=False)
```

profile of v0, /device:TPU:13, one launch (start us, length us, event | category | flops | bytes accessed | tf_op | source)
XLA Modules:
  0.0 1311.0 jit_solution(4099106619607151137)
XLA Ops:
  22.2 6.0 all-gather.14.cloned.1.call-done
  28.2 3.8 fusion
  43.5 99.3 %all-gather.16.cloned.1.call-done = bf16[2,1024,2048]{2,1,0:T(8,128)(2,1)} async-done(((bf16[2,64,2048]{2,1,0:T(8,128)(2,1)}), bf16[2,1024,2048]{2,1,0:T(8,128)(2,1)}) %all-gather.16.cloned.1.call-update) | async-done | bytes 8388624 | tf_op jit(solution)/shard_map/all_gather | solution.py:123
  142.8 5.9 fusion.95
  148.7 6.4 copy.60
  155.1 6.2 copy.63
  174.2 5.0 all-gather.20.cloned.1.call-done
  179.1 4.8 convolution_add_fusion
  183.9 17.7 %all-gather.22.cloned.1.call-done = bf16[4096,1024]{1,0:T(8,128)(2,1)} async-done(((bf16[2048,1024]{1,0:T(8,128)(2,1)}), bf16[4096,1024]{1,0:T(8,128)(2,1)}) %all-gather.22.cloned.1.call-update) | async-done | bytes 8388624 | tf_op jit(solution)/shard_map/all_gather | solution.py:102
  201.6 7.6 fusion.101
  227.7 5.1 multiply_convert_fusion
  235.5 5.4 copy.74
  243.8 4.6 multiply_convert_fusion.1
  252.4 5.4 copy.72
  257.9 5.2 fusion.14
  263.1 5.4 copy.76
  268.6 5.2 fusion.12
  273.8 5.4 copy.78
  292.4 42.6 %reduce-scatter.11.cloned.1.call-done = f32[2,64,512]{2,1,0:T(8,128)} async-done(((f32[2,1024,512]{2,1,0:T(8,128)}), f32[2,64,512]{2,1,0:T(8,128)}) %reduce-scatter.11.cloned.1.call-update) | async-done | bytes 262160 | tf_op jit(solution)/shard_map/reduce_scatter | solution.py:252
  336.0 96.1 %reduce-scatter.9.cloned.1.call-done = f32[2,64,512]{2,1,0:T(8,128)} async-done(((f32[2,1024,512]{2,1,0:T(8,128)}), f32[2,64,512]{2,1,0:T(8,128)}) %reduce-scatter.9.cloned.1.call-update) | async-done | bytes 262160 | tf_op jit(solution)/shard_map/reduce_scatter | solution.py:252
  433.8 95.4 %reduce-scatter.13.cloned.1.call-done = f32[2,64,512]{2,1,0:T(8,128)} async-done(((f32[2,1024,512]{2,1,0:T(8,128)}), f32[2,64,512]{2,1,0:T(8,128)}) %reduce-scatter.13.cloned.1.call-update) | async-done | bytes 262160 | tf_op jit(solution)/shard_map/reduce_scatter | solution.py:258
  530.8 95.4 %reduce-scatter.15.cloned.1.call-done = f32[2,64,512]{2,1,0:T(8,128)} async-done(((f32[2,1024,512]{2,1,0:T(8,128)}), f32[2,64,512]{2,1,0:T(8,128)}) %reduce-scatter.15.cloned.1.call-update) | async-done | bytes 262160 | tf_op jit(solution)/shard_map/reduce_scatter | solution.py:258
  629.9 7.4 fusion.70
  638.0 9.4 fusion.66
  647.4 9.1 fusion.93
  661.7 5.7 fusion.48
  667.5 5.2 multiply_reduce_fusion.1
  672.7 41.6 %all-reduce.9 = (f32[1024]{0:T(1024)S(1)}, f32[1024]{0:T(1024)S(1)}, f32[1024]{0:T(1024)S(1)}, f32[1024]{0:T(1024)S(1)}, f32[1024]{0:T(1024)S(1)}, /*index=5*/f3...) all-reduce(f32[1024]{0:T(1024)S(1)} %get-tuple-element.17, ...), channel_id=6, replica_groups=mesh['ctx'=16,'fsdp'=2] {'ctx','fsdp'}, use_global_device_ids=true, to_apply=%region_16.17.clone | all-reduce | flops 12288 | bytes 98304
  720.6 19.2 %reduce-scatter.19.cloned.1.call-done = f32[32,1024]{1,0:T(8,128)} async-done(((f32[1024,1024]{1,0:T(8,128)}), f32[32,1024]{1,0:T(8,128)}) %reduce-scatter.19.cloned.1.call-update) | async-done | bytes 131088 | tf_op jit(solution)/shard_map/reduce_scatter | solution.py:296
  739.8 188.1 %reduce-scatter.17.cloned.1.call-done = f32[32,3072]{1,0:T(8,128)} async-done(((f32[1024,3072]{1,0:T(8,128)}), f32[32,3072]{1,0:T(8,128)}) %reduce-scatter.17.cloned.1.call-update) | async-done | bytes 393232 | tf_op jit(solution)/shard_map/reduce_scatter | solution.py:289
  927.9 188.8 %reduce-scatter.21.cloned.1.call-done = f32[32,4096]{1,0:T(8,128)} async-done(((f32[1024,4096]{1,0:T(8,128)}), f32[32,4096]{1,0:T(8,128)}) %reduce-scatter.21.cloned.1.call-update) | async-done | bytes 524304 | tf_op jit(solution)/shard_map/reduce_scatter | solution.py:188
  1116.8 187.5 %reduce-scatter.23.cloned.1.call-done = f32[128,1024]{1,0:T(8,128)} async-done(((f32[4096,1024]{1,0:T(8,128)}), f32[128,1024]{1,0:T(8,128)}) %reduce-scatter.23.cloned.1.call-update) | async-done | bytes 524304 | tf_op jit(solution)/shard_map/reduce_scatter | solution.py:192
  (220 shorter events, 100.3 us)
Async XLA Ops:
  7.2 21.0 %all-gather.14.cloned.1.call-start = ((), (), s32[]{:S(2)}) async-start(), calls=%async_computation.8 | async-start | bytes 9437184 | tf_op jit(solution)/shard_map/all_gather | solution.py:93
  7.9 134.9 %all-gather.16.cloned.1.call-start = ((), (), s32[]{:S(2)}) async-start(), calls=%async_computation.9 | async-start | bytes 8912896 | tf_op jit(solution)/shard_map/all_gather | solution.py:123
  14.5 7.6 copy-start.36
  15.7 6.4 copy-start.38
  22.1 9.8 copy-start.11
  32.8 138.7 %all-gather.18.cloned.1.call-start = ((), (), s32[]{:S(2)}) async-start(), calls=%async_computation.10 | async-start | bytes 3145728 | tf_op jit(solution)/shard_map/all_gather | solution.py:96
  33.6 5.3 copy-start.41
  33.6 7.1 copy-start.42
  33.6 9.1 copy-start.33
  33.6 145.5 %all-gather.20.cloned.1.call-start = ((), (), s32[]{:S(2)}) async-start(), calls=%async_computation.11 | async-start | bytes 12582912 | tf_op jit(solution)/shard_map/all_gather | solution.py:100
  34.2 167.4 %all-gather.22.cloned.1.call-start = ((), (), s32[]{:S(2)}) async-start(), calls=%async_computation.12 | async-start | bytes 12582912 | tf_op jit(solution)/shard_map/all_gather | solution.py:102
  34.8 300.2 %reduce-scatter.11.cloned.1.call-start = ((), (), s32[]{:S(2)}) async-start(), calls=%async_computation.14 | async-start | bytes 4456448 | tf_op jit(solution)/shard_map/reduce_scatter | solution.py:252
  43.5 117.9 %copy-start.14 = (bf16[2,64,8,64]{3,2,1,0:T(8,128)(2,1)}, bf16[2,64,8,64]{3,2,1,0:T(8,128)(2,1)S(1)}, u32[]{:S(2)}) copy-start(bf16[2,64,8,64]{3,2,1,0:T(8,128)(2,1)S(1)} %get-tuple-element.43) | copy-start | bytes 393220
  43.5 120.3 %copy-start.21 = (bf16[2,64,8,64]{3,2,1,0:T(8,128)(2,1)}, bf16[2,64,8,64]{3,2,1,0:T(8,128)(2,1)S(1)}, u32[]{:S(2)}) copy-start(bf16[2,64,8,64]{3,2,1,0:T(8,128)(2,1)S(1)} %get-tuple-element.42) | copy-start | bytes 393220
  171.5 7.7 copy-start.7
  174.1 35.1 %copy-start.27 = (f32[128]{0:T(128)}, f32[128]{0:T(128)S(1)}, u32[]{:S(2)}) copy-start(f32[128]{0:T(128)S(1)} %add_rsqrt_fusion.1) | copy-start | bytes 1540
  179.1 22.4 %copy-start.12 = (bf16[2,64,1024]{2,1,0:T(8,128)(2,1)S(1)}, bf16[2,64,1024]{2,1,0:T(8,128)(2,1)}, u32[]{:S(2)}) copy-start(bf16[2,64,1024]{2,1,0:T(8,128)(2,1)} %param.18) | copy-start | bytes 786436
  201.6 7.7 copy-start
  240.9 191.1 %reduce-scatter.9.cloned.1.call-start = ((), (), s32[]{:S(2)}) async-start(), calls=%async_computation.13 | async-start | bytes 4456448 | tf_op jit(solution)/shard_map/reduce_scatter | solution.py:252
  243.8 5.9 copy-start.22
  257.9 271.3 %reduce-scatter.13.cloned.1.call-start = ((), (), s32[]{:S(2)}) async-start(), calls=%async_computation.15 | async-start | bytes 4456448 | tf_op jit(solution)/shard_map/reduce_scatter | solution.py:258
  268.6 357.7 %reduce-scatter.15.cloned.1.call-start = ((), (), s32[]{:S(2)}) async-start(), calls=%async_computation.16 | async-start | bytes 4456448 | tf_op jit(solution)/shard_map/reduce_scatter | solution.py:258
  279.3 460.6 %reduce-scatter.19.cloned.1.call-start = ((), (), s32[]{:S(2)}) async-start(), calls=%async_computation.18 | async-start | bytes 4325376 | tf_op jit(solution)/shard_map/reduce_scatter | solution.py:296
  283.1 644.8 %reduce-scatter.17.cloned.1.call-start = ((), (), s32[]{:S(2)}) async-start(), calls=%async_computation.17 | async-start | bytes 12976128 | tf_op jit(solution)/shard_map/reduce_scatter | solution.py:289
  637.3 479.4 %reduce-scatter.21.cloned.1.call-start = ((), (), s32[]{:S(2)}) async-start(), calls=%async_computation.19 | async-start | bytes 17301504 | tf_op jit(solution)/shard_map/reduce_scatter | solution.py:188
  647.4 656.9 %reduce-scatter.23.cloned.1.call-start = ((), (), s32[]{:S(2)}) async-start(), calls=%async_computation.20 | async-start | bytes 17301504 | tf_op jit(solution)/shard_map/reduce_scatter | solution.py:192
  661.7 5.7 copy-start.23
  661.7 5.7 copy-start.25
  661.7 5.7 copy-start.26
  661.7 5.7 copy-start.37
  661.7 5.7 copy-start.39
  667.4 5.2 copy-start.29
  (26 other events, 80.0 us)
Sparse Core Ops, SparseCore 0:
  9.5 18.5 all-gather.13
  32.9 109.8 all-gather.15
  144.3 12.2 all-gather.17
  158.1 21.0 all-gather.19
  180.5 21.0 all-gather.21
  241.1 93.9 reduce-scatter.10
  337.3 94.7 reduce-scatter.8
  434.4 94.7 reduce-scatter.12
  531.5 94.7 reduce-scatter.14
  629.0 110.8 reduce-scatter.18
  746.4 181.4 reduce-scatter.16
  930.7 186.0 reduce-scatter.20
  1119.6 184.5 reduce-scatter.22
where the time goes:
time: 1320 us; the launch traced here: 1310 us
  waiting for transfers between devices  1040 us (79%)
  matrix products  100 us (8%)
  local copies, waits for them, and re-layouts  77.6 us (6%)
  blocking collectives  58.6 us (4%)
  other arithmetic  15.4 us (1%)
  between operations  14.8 us (1%)
    reduce_scatter x2, waiting for transfers between devices, body(): lax.psum_scatter(value_term.reshape(groups, length, half_heads * head), '...  191 us
    reduce_scatter x1, waiting for transfers between devices, body(): lax.psum_scatter(grad_expand, ('ctx', 'fsdp'), scatter_dimension=0, tiled...  189 us
    reduce_scatter x1, waiting for transfers between devices, body(): lax.psum_scatter(grad_mix, ('ctx', 'fsdp'), scatter_dimension=0, tiled=True)  188 us
    reduce_scatter x1, waiting for transfers between devices, body(): lax.psum_scatter(grad_reduce, ('ctx', 'fsdp'), scatter_dimension=0, tiled...  188 us
    reduce_scatter x2, waiting for transfers between devices, body(): lax.psum_scatter(key_term.reshape(groups, length, half_heads * head), 'ct...  139 us
    all_gather x1, waiting for transfers between devices, body(): pairs = lax.all_gather(local_pairs, 'ctx', axis=1, tiled=True)  99.3 us
    unnamed x1, blocking collectives  41.6 us
  transfers between devices with their start and end apart: 13, of which 12 were waited for; matrix products, arithmetic and copies ran while one was open for 11% of the time, Pallas kernels for 0%

commit v1 on v0

--- a/solution.py
+++ b/solution.py
@@ -8,6 +8,19 @@
 EPSILON = 1e-05
 CUBIC = 0.044715
 ROOT = math.sqrt(2.0 / math.pi)
+
+
+def gather_around(x, axis, dim):
+    ways = lax.axis_size(axis)
+    up = [(d, (d + 1) % ways) for d in range(ways)]
+    down = [(d, (d - 1) % ways) for d in range(ways)]
+    earlier, later = ([x], [x])
+    for _ in range(ways // 2):
+        earlier.append(lax.ppermute(earlier[-1], axis, up))
+    for _ in range((ways - 1) // 2):
+        later.append(lax.ppermute(later[-1], axis, down))
+    line = jnp.concatenate([*earlier[::-1], *later[1:]], axis=dim)
+    return jnp.roll(line, (lax.axis_index(axis) - ways // 2) * x.shape[dim], axis=dim)
 
 
 def gelu_value(pre):
@@ -120,7 +133,7 @@
     )
     queries = mixed[:, :model].reshape(groups, width, heads, head)
     local_pairs = mixed[:, model:].reshape(groups, width, 2 * model)
-    pairs = lax.all_gather(local_pairs, "ctx", axis=1, tiled=True)
+    pairs = gather_around(local_pairs, "ctx", 1)
     keys = pairs[:, :, :model].reshape(groups, length, heads, head)
     values = pairs[:, :, model:].reshape(groups, length, heads, head)
     context_parts, log_parts = ([], [])

time: 1320 us -> 1420 us (1.076)
  local copies, waits for them, and re-layouts: 77.6 us -> 119 us
  waiting for transfers between devices: 1040 us -> 1080 us
    ppermute x0 -> x15, waiting for transfers between devices: none -> 141 us  [the longest x7 105 us: gather_around(): later.append(lax.ppermute(later[-1], axis, down))]
    all_gather x1 -> x0, waiting for transfers between devices: 99.3 us -> none  [body(): pairs = lax.all_gather(local_pairs, 'ctx', axis=1, tiled=True)]
    unnamed x110 -> x163, local copies, waits for them, and re-layouts: 16.9 us -> 56.6 us
    all_gather x1, waiting for transfers between devices: 17.7 us -> 0.02 us  [body(): lax.all_gather(w_reduce, 'fsdp', axis=0, tiled=True)]
  transfers between devices with their start and end apart: 13 -> 27, of which waited for: 12 -> 19; matrix products, arithmetic and copies ran while one was open for 11% -> 13% of each run, Pallas kernels for 0% -> 0%
where the time goes in v1:
time: 1420 us; the launch traced here: 1410 us
  waiting for transfers between devices  1080 us (76%)
  local copies, waits for them, and re-layouts  119 us (8%)
  matrix products  100 us (7%)
  blocking collectives  69.7 us (5%)
  between operations  15.3 us (1%)
  starting transfers between devices  14.7 us (1%)
    reduce_scatter x2, waiting for transfers between devices, body(): lax.psum_scatter(value_term.reshape(groups, length, half_heads * head), '...  191 us
    reduce_scatter x1, waiting for transfers between devices, body(): lax.psum_scatter(grad_expand, ('ctx', 'fsdp'), scatter_dimension=0, tiled...  189 us
    reduce_scatter x1, waiting for transfers between devices, body(): lax.psum_scatter(grad_mix, ('ctx', 'fsdp'), scatter_dimension=0, tiled=True)  188 us
    reduce_scatter x1, waiting for transfers between devices, body(): lax.psum_scatter(grad_reduce, ('ctx', 'fsdp'), scatter_dimension=0, tiled...  187 us
    reduce_scatter x2, waiting for transfers between devices, body(): lax.psum_scatter(key_term.reshape(groups, length, half_heads * head), 'ct...  149 us
    ppermute x7, waiting for transfers between devices, gather_around(): later.append(lax.ppermute(later[-1], axis, down))  105 us
    unnamed x163, local copies, waits for them, and re-layouts  56.6 us
    unnamed x1, blocking collectives  41.7 us
  transfers between devices with their start and end apart: 27, of which 19 were waited for; matrix products, arithmetic and copies ran while one was open for 13% of the time, Pallas kernels for 0%

profile of v1, /device:TPU:13, one launch (start us, length us, event | category | flops | bytes accessed | tf_op | source)
XLA Modules:
  0.0 1408.9 jit_solution(8551016068747936742)
XLA Ops:
  18.2 10.1 all-gather.13.cloned.1.call-done
  33.4 13.0 collective-permute-done
  48.7 10.9 collective-permute-done.1
  59.9 24.6 %collective-permute-done.8 = bf16[2,64,2048]{2,1,0:T(8,128)(2,1)S(1)} collective-permute-done((bf16[2,64,2048]{2,1,0:T(8,128)(2,1)S(1)}, bf16[2,64,2048]{2,1,0:T(8,128)(2,1)S(1)}, u32[]{:S(2)}, u32[]{:S(2)}) %collective-permute-start.8) | collective-permute-done | bytes 524320 | tf_op jit(solution)/shard_map/ppermute | solution.py:21
  85.9 34.0 %collective-permute-done.9 = bf16[2,64,2048]{2,1,0:T(8,128)(2,1)S(1)} collective-permute-done((bf16[2,64,2048]{2,1,0:T(8,128)(2,1)S(1)}, bf16[2,64,2048]{2,1,0:T(8,128)(2,1)S(1)}, u32[]{:S(2)}, u32[]{:S(2)}) %collective-permute-start.9) | collective-permute-done | bytes 524320 | tf_op jit(solution)/shard_map/ppermute | solution.py:21
  122.2 22.9 %collective-permute-done.10 = bf16[2,64,2048]{2,1,0:T(8,128)(2,1)} collective-permute-done((bf16[2,64,2048]{2,1,0:T(8,128)(2,1)S(1)}, bf16[2,64,2048]{2,1,0:T(8,128)(2,1)}, u32[]{:S(2)}, u32[]{:S(2)}) %collective-permute-start.10) | collective-permute-done | bytes 524320 | tf_op jit(solution)/shard_map/ppermute | solution.py:21
  146.6 16.5 %collective-permute-done.11 = bf16[2,64,2048]{2,1,0:T(8,128)(2,1)} collective-permute-done((bf16[2,64,2048]{2,1,0:T(8,128)(2,1)}, bf16[2,64,2048]{2,1,0:T(8,128)(2,1)}, u32[]{:S(2)}, u32[]{:S(2)}) %collective-permute-start.11) | collective-permute-done | bytes 524320 | tf_op jit(solution)/shard_map/ppermute | solution.py:21
  169.5 6.7 collective-permute-done.12
  177.4 8.1 collective-permute-done.6
  187.8 12.7 all-gather.4
  251.5 7.8 constant_dynamic-slice_fusion.2
  259.4 6.3 copy.60
  265.7 6.2 copy.63
  288.5 7.6 fusion.100
  322.1 5.4 copy.74
  339.1 5.3 copy.72
  344.5 5.4 fusion.14
  349.9 5.4 copy.76
  360.7 5.5 copy.78
  379.4 52.8 %reduce-scatter.11.cloned.1.call-done = f32[2,64,512]{2,1,0:T(8,128)} async-done(((f32[2,1024,512]{2,1,0:T(8,128)}), f32[2,64,512]{2,1,0:T(8,128)}) %reduce-scatter.11.cloned.1.call-update) | async-done | bytes 262160 | tf_op jit(solution)/shard_map/reduce_scatter | solution.py:265
  433.1 95.9 %reduce-scatter.9.cloned.1.call-done = f32[2,64,512]{2,1,0:T(8,128)} async-done(((f32[2,1024,512]{2,1,0:T(8,128)}), f32[2,64,512]{2,1,0:T(8,128)}) %reduce-scatter.9.cloned.1.call-update) | async-done | bytes 262160 | tf_op jit(solution)/shard_map/reduce_scatter | solution.py:265
  530.8 95.3 %reduce-scatter.13.cloned.1.call-done = f32[2,64,512]{2,1,0:T(8,128)} async-done(((f32[2,1024,512]{2,1,0:T(8,128)}), f32[2,64,512]{2,1,0:T(8,128)}) %reduce-scatter.13.cloned.1.call-update) | async-done | bytes 262160 | tf_op jit(solution)/shard_map/reduce_scatter | solution.py:271
  627.8 95.4 %reduce-scatter.15.cloned.1.call-done = f32[2,64,512]{2,1,0:T(8,128)} async-done(((f32[2,1024,512]{2,1,0:T(8,128)}), f32[2,64,512]{2,1,0:T(8,128)}) %reduce-scatter.15.cloned.1.call-update) | async-done | bytes 262160 | tf_op jit(solution)/shard_map/reduce_scatter | solution.py:271
  726.9 7.4 fusion.70
  734.9 9.4 fusion.66
  744.4 9.1 fusion.93
  758.8 5.7 fusion.48
  769.8 41.7 %all-reduce.9 = (f32[1024]{0:T(1024)S(1)}, f32[1024]{0:T(1024)S(1)}, f32[1024]{0:T(1024)S(1)}, f32[1024]{0:T(1024)S(1)}, f32[1024]{0:T(1024)S(1)}, /*index=5*/f3...) all-reduce(f32[1024]{0:T(1024)S(1)} %get-tuple-element.17, ...), channel_id=6, replica_groups=mesh['ctx'=16,'fsdp'=2] {'ctx','fsdp'}, use_global_device_ids=true, to_apply=%region_16.17.clone | all-reduce | flops 12288 | bytes 98304
  817.7 19.2 %reduce-scatter.19.cloned.1.call-done = f32[32,1024]{1,0:T(8,128)} async-done(((f32[1024,1024]{1,0:T(8,128)}), f32[32,1024]{1,0:T(8,128)}) %reduce-scatter.19.cloned.1.call-update) | async-done | bytes 131088 | tf_op jit(solution)/shard_map/reduce_scatter | solution.py:309
  836.9 188.4 %reduce-scatter.17.cloned.1.call-done = f32[32,3072]{1,0:T(8,128)} async-done(((f32[1024,3072]{1,0:T(8,128)}), f32[32,3072]{1,0:T(8,128)}) %reduce-scatter.17.cloned.1.call-update) | async-done | bytes 393232 | tf_op jit(solution)/shard_map/reduce_scatter | solution.py:302
  1025.3 189.1 %reduce-scatter.21.cloned.1.call-done = f32[32,4096]{1,0:T(8,128)} async-done(((f32[1024,4096]{1,0:T(8,128)}), f32[32,4096]{1,0:T(8,128)}) %reduce-scatter.21.cloned.1.call-update) | async-done | bytes 524304 | tf_op jit(solution)/shard_map/reduce_scatter | solution.py:201
  1214.4 187.4 %reduce-scatter.23.cloned.1.call-done = f32[128,1024]{1,0:T(8,128)} async-done(((f32[4096,1024]{1,0:T(8,128)}), f32[128,1024]{1,0:T(8,128)}) %reduce-scatter.23.cloned.1.call-update) | async-done | bytes 524304 | tf_op jit(solution)/shard_map/reduce_scatter | solution.py:205
  (301 shorter events, 182.4 us)
Async XLA Ops:
  7.2 21.0 %all-gather.13.cloned.1.call-start = ((), (), s32[]{:S(2)}) async-start(), calls=%async_computation.8 | async-start | bytes 9437184 | tf_op jit(solution)/shard_map/all_gather | solution.py:106
  8.0 273.2 %all-gather.15.cloned.1.call-start = ((), (), s32[]{:S(2)}) async-start(), calls=%async_computation.9 | async-start | bytes 3145728 | tf_op jit(solution)/shard_map/all_gather | solution.py:109
  8.7 274.9 %all-gather.17.cloned.1.call-start = ((), (), s32[]{:S(2)}) async-start(), calls=%async_computation.10 | async-start | bytes 12582912 | tf_op jit(solution)/shard_map/all_gather | solution.py:113
  9.4 279.0 %all-gather.19.cloned.1.call-start = ((), (), s32[]{:S(2)}) async-start(), calls=%async_computation.11 | async-start | bytes 12582912 | tf_op jit(solution)/shard_map/all_gather | solution.py:115
  32.0 155.7 %copy-start.40 = (s32[2,1024]{1,0:T(2,128)S(1)}, s32[2,1024]{1,0:T(2,128)}, u32[]{:S(2)}) copy-start(s32[2,1024]{1,0:T(2,128)} %param.20) | copy-start | bytes 24580
  32.0 155.8 %copy-start.51 = (bf16[512]{0:T(512)(128)(2,1)S(1)}, bf16[512]{0:T(512)(128)(2,1)}, u32[]{:S(2)}) copy-start(bf16[512]{0:T(512)(128)(2,1)} %param.27) | copy-start | bytes 3076
  32.0 168.4 %copy-start.42 = (bf16[2048]{0:T(1024)(128)(2,1)S(1)}, bf16[2048]{0:T(1024)(128)(2,1)}, u32[]{:S(2)}) copy-start(bf16[2048]{0:T(1024)(128)(2,1)} %param.31) | copy-start | bytes 12292
  32.1 170.9 %copy-start.52 = (bf16[512]{0:T(512)(128)(2,1)S(1)}, bf16[512]{0:T(512)(128)(2,1)}, u32[]{:S(2)}) copy-start(bf16[512]{0:T(512)(128)(2,1)} %param.29) | copy-start | bytes 3076
  32.1 172.7 %copy-start.53 = (bf16[512]{0:T(512)(128)(2,1)S(1)}, bf16[512]{0:T(512)(128)(2,1)}, u32[]{:S(2)}) copy-start(bf16[512]{0:T(512)(128)(2,1)} %param.28) | copy-start | bytes 3076
  32.1 14.2 %collective-permute-start = (bf16[2,64,2048]{2,1,0:T(8,128)(2,1)S(1)}, bf16[2,64,2048]{2,1,0:T(8,128)(2,1)S(1)}, u32[]{:S(2)}, u32[]{:S(2)}) collective-permute-start(bf16[2,64,2048]{2,1,0:T(8,128)(2,1)S(1)} %bitcast.101), channel_id=1, source_target_pairs={{0,2},{2,4},{4,6},{6,8},{8,10},{10,12},{12,14},{14,16},{16,18},{18... | collective-permute-start | bytes 1572872 | tf_op jit(solution)/shard_map/ppermute | solution.py:19
  46.3 13.3 collective-permute-start.1
  46.6 37.8 %collective-permute-start.8 = (bf16[2,64,2048]{2,1,0:T(8,128)(2,1)S(1)}, bf16[2,64,2048]{2,1,0:T(8,128)(2,1)S(1)}, u32[]{:S(2)}, u32[]{:S(2)}) collective-permute-start(bf16[2,64,2048]{2,1,0:T(8,128)(2,1)S(1)} %bitcast.102), channel_id=1, source_target_pairs={{0,30},{2,0},{4,2},{6,4},{8,6},{10,8},{12,10},{14,12},{16,14},{18,... | collective-permute-start | bytes 1572872 | tf_op jit(solution)/shard_map/ppermute | solution.py:21
  59.6 24.8 %collective-permute-start.2 = (bf16[2,64,2048]{2,1,0:T(8,128)(2,1)S(1)}, bf16[2,64,2048]{2,1,0:T(8,128)(2,1)S(1)}, u32[]{:S(2)}, u32[]{:S(2)}) collective-permute-start(bf16[2,64,2048]{2,1,0:T(8,128)(2,1)S(1)} %collective-permute-done.1), channel_id=1, source_target_pairs={{0,2},{2,4},{4,6},{6,8},{8,10},{10,12},{12,14},{14,16},{16,18},{18... | collective-permute-start | bytes 1572872 | tf_op jit(solution)/shard_map/ppermute | solution.py:19
  84.4 35.4 %collective-permute-start.9 = (bf16[2,64,2048]{2,1,0:T(8,128)(2,1)S(1)}, bf16[2,64,2048]{2,1,0:T(8,128)(2,1)S(1)}, u32[]{:S(2)}, u32[]{:S(2)}) collective-permute-start(bf16[2,64,2048]{2,1,0:T(8,128)(2,1)S(1)} %collective-permute-done.8), channel_id=1, source_target_pairs={{0,30},{2,0},{4,2},{6,4},{8,6},{10,8},{12,10},{14,12},{16,14},{18,... | collective-permute-start | bytes 1572872 | tf_op jit(solution)/shard_map/ppermute | solution.py:21
  84.5 36.2 %collective-permute-start.3 = (bf16[2,64,2048]{2,1,0:T(8,128)(2,1)S(1)}, bf16[2,64,2048]{2,1,0:T(8,128)(2,1)S(1)}, u32[]{:S(2)}, u32[]{:S(2)}) collective-permute-start(bf16[2,64,2048]{2,1,0:T(8,128)(2,1)S(1)} %collective-permute-done.2), channel_id=1, source_target_pairs={{0,2},{2,4},{4,6},{6,8},{8,10},{10,12},{12,14},{14,16},{16,18},{18... | collective-permute-start | bytes 1572872 | tf_op jit(solution)/shard_map/ppermute | solution.py:19
  120.7 24.3 %collective-permute-start.10 = (bf16[2,64,2048]{2,1,0:T(8,128)(2,1)S(1)}, bf16[2,64,2048]{2,1,0:T(8,128)(2,1)}, u32[]{:S(2)}, u32[]{:S(2)}) collective-permute-start(bf16[2,64,2048]{2,1,0:T(8,128)(2,1)S(1)} %collective-permute-done.9), channel_id=1, source_target_pairs={{0,30},{2,0},{4,2},{6,4},{8,6},{10,8},{12,10},{14,12},{16,14},{18,... | collective-permute-start | bytes 1572872 | tf_op jit(solution)/shard_map/ppermute | solution.py:21
  120.7 24.3 %collective-permute-start.4 = (bf16[2,64,2048]{2,1,0:T(8,128)(2,1)S(1)}, bf16[2,64,2048]{2,1,0:T(8,128)(2,1)}, u32[]{:S(2)}, u32[]{:S(2)}) collective-permute-start(bf16[2,64,2048]{2,1,0:T(8,128)(2,1)S(1)} %collective-permute-done.3), channel_id=1, source_target_pairs={{0,2},{2,4},{4,6},{6,8},{8,10},{10,12},{12,14},{14,16},{16,18},{18... | collective-permute-start | bytes 1572872 | tf_op jit(solution)/shard_map/ppermute | solution.py:19
  145.0 18.1 %collective-permute-start.11 = (bf16[2,64,2048]{2,1,0:T(8,128)(2,1)}, bf16[2,64,2048]{2,1,0:T(8,128)(2,1)}, u32[]{:S(2)}, u32[]{:S(2)}) collective-permute-start(bf16[2,64,2048]{2,1,0:T(8,128)(2,1)} %collective-permute-done.10), channel_id=1, source_target_pairs={{0,30},{2,0},{4,2},{6,4},{8,6},{10,8},{12,10},{14,12},{16,14},{18,... | collective-permute-start | bytes 1572872 | tf_op jit(solution)/shard_map/ppermute | solution.py:21
  145.0 21.8 %collective-permute-start.5 = (bf16[2,64,2048]{2,1,0:T(8,128)(2,1)}, bf16[2,64,2048]{2,1,0:T(8,128)(2,1)}, u32[]{:S(2)}, u32[]{:S(2)}) collective-permute-start(bf16[2,64,2048]{2,1,0:T(8,128)(2,1)} %collective-permute-done.4), channel_id=1, source_target_pairs={{0,2},{2,4},{4,6},{6,8},{8,10},{10,12},{12,14},{14,16},{16,18},{18... | collective-permute-start | bytes 1572872 | tf_op jit(solution)/shard_map/ppermute | solution.py:19
  146.5 285.6 %reduce-scatter.11.cloned.1.call-start = ((), (), s32[]{:S(2)}) async-start(), calls=%async_computation.13 | async-start | bytes 4456448 | tf_op jit(solution)/shard_map/reduce_scatter | solution.py:265
  163.1 13.1 collective-permute-start.12
  166.8 18.7 %collective-permute-start.6 = (bf16[2,64,2048]{2,1,0:T(8,128)(2,1)}, bf16[2,64,2048]{2,1,0:T(8,128)(2,1)}, u32[]{:S(2)}, u32[]{:S(2)}) collective-permute-start(bf16[2,64,2048]{2,1,0:T(8,128)(2,1)} %collective-permute-done.5), channel_id=1, source_target_pairs={{0,2},{2,4},{4,6},{6,8},{8,10},{10,12},{12,14},{14,16},{16,18},{18... | collective-permute-start | bytes 1572872 | tf_op jit(solution)/shard_map/ppermute | solution.py:19
  176.2 31.1 %collective-permute-start.13 = (bf16[2,64,2048]{2,1,0:T(8,128)(2,1)}, bf16[2,64,2048]{2,1,0:T(8,128)(2,1)}, u32[]{:S(2)}, u32[]{:S(2)}) collective-permute-start(bf16[2,64,2048]{2,1,0:T(8,128)(2,1)} %collective-permute-done.12), channel_id=1, source_target_pairs={{0,30},{2,0},{4,2},{6,4},{8,6},{10,8},{12,10},{14,12},{16,14},{18,... | collective-permute-start | bytes 1572872 | tf_op jit(solution)/shard_map/ppermute | solution.py:21
  185.5 22.5 %collective-permute-start.7 = (bf16[2,64,2048]{2,1,0:T(8,128)(2,1)}, bf16[2,64,2048]{2,1,0:T(8,128)(2,1)}, u32[]{:S(2)}, u32[]{:S(2)}) collective-permute-start(bf16[2,64,2048]{2,1,0:T(8,128)(2,1)} %collective-permute-done.6), channel_id=1, source_target_pairs={{0,2},{2,4},{4,6},{6,8},{8,10},{10,12},{12,14},{14,16},{16,18},{18... | collective-permute-start | bytes 1572872 | tf_op jit(solution)/shard_map/ppermute | solution.py:19
  207.3 21.6 %collective-permute-start.14 = (bf16[2,64,2048]{2,1,0:T(8,128)(2,1)}, bf16[2,64,2048]{2,1,0:T(8,128)(2,1)S(1)}, u32[]{:S(2)}, u32[]{:S(2)}) collective-permute-start(bf16[2,64,2048]{2,1,0:T(8,128)(2,1)} %collective-permute-done.13), channel_id=1, source_target_pairs={{0,30},{2,0},{4,2},{6,4},{8,6},{10,8},{12,10},{14,12},{16,14},{18,... | collective-permute-start | bytes 1572872 | tf_op jit(solution)/shard_map/ppermute | solution.py:21
  327.5 201.6 %reduce-scatter.9.cloned.1.call-start = ((), (), s32[]{:S(2)}) async-start(), calls=%async_computation.12 | async-start | bytes 4456448 | tf_op jit(solution)/shard_map/reduce_scatter | solution.py:265
  344.4 281.7 %reduce-scatter.13.cloned.1.call-start = ((), (), s32[]{:S(2)}) async-start(), calls=%async_computation.14 | async-start | bytes 4456448 | tf_op jit(solution)/shard_map/reduce_scatter | solution.py:271
  355.4 367.9 %reduce-scatter.15.cloned.1.call-start = ((), (), s32[]{:S(2)}) async-start(), calls=%async_computation.15 | async-start | bytes 4456448 | tf_op jit(solution)/shard_map/reduce_scatter | solution.py:271
  366.2 470.7 %reduce-scatter.19.cloned.1.call-start = ((), (), s32[]{:S(2)}) async-start(), calls=%async_computation.17 | async-start | bytes 4325376 | tf_op jit(solution)/shard_map/reduce_scatter | solution.py:309
  370.0 655.3 %reduce-scatter.17.cloned.1.call-start = ((), (), s32[]{:S(2)}) async-start(), calls=%async_computation.16 | async-start | bytes 12976128 | tf_op jit(solution)/shard_map/reduce_scatter | solution.py:302
  734.3 480.0 %reduce-scatter.21.cloned.1.call-start = ((), (), s32[]{:S(2)}) async-start(), calls=%async_computation.18 | async-start | bytes 17301504 | tf_op jit(solution)/shard_map/reduce_scatter | solution.py:201
  744.4 657.4 %reduce-scatter.23.cloned.1.call-start = ((), (), s32[]{:S(2)}) async-start(), calls=%async_computation.19 | async-start | bytes 17301504 | tf_op jit(solution)/shard_map/reduce_scatter | solution.py:205
  (51 other events, 593.7 us)
Sparse Core Ops, SparseCore 0:
  9.6 18.5 all-gather.12
  29.7 11.7 all-gather.14
  43.1 21.0 all-gather.16
  146.6 20.6 all-gather.18
  327.6 104.5 reduce-scatter.10
  434.3 94.7 reduce-scatter.8
  531.4 94.7 reduce-scatter.12
  628.4 94.7 reduce-scatter.14
  726.1 110.8 reduce-scatter.18
  843.4 181.8 reduce-scatter.16
  1028.2 186.1 reduce-scatter.20
  1217.1 184.6 reduce-scatter.22
